TPU v7x, 128 devices: a whole 4x4x4 slice. The times are simulated.
128 devices in a mesh: ent: 32 (over x, z, y_lo), qry: 4 (over y_hi, core).
Axes of the slice: x: 4, y: 4 (y_hi: 2, y_lo: 2; y = y_hi * 2 + y_lo), z: 4, core: 2. Of those that a mesh axis runs over, the one named last changes fastest.
Arguments:
- ent_emb: bfloat16 [65536, 512], P('ent'), may hold values from -1 to 1
- ent_tan: bfloat16 [65536, 512], P('ent'), may hold values from -0.25 to 0.25
- qry_emb: bfloat16 [4096, 512], P(('qry', 'ent')), may hold values from -6 to 6
- qry_tan: bfloat16 [4096, 512], P(('qry', 'ent')), may hold values from -6 to 6
- tails: int32 [4096, 4], P('qry'), may hold values from 0 to 65535
Outputs:
- ent_gnvp: float32 [65536, 512], P(('ent', 'qry'))
- ent_grad: float32 [65536, 512], P(('ent', 'qry'))
- qry_gnvp: float32 [4096, 512], P(('qry', 'ent'))
- qry_grad: float32 [4096, 512], P(('qry', 'ent'))
All inputs are finite; a program needn't handle non-finite values.
Results may differ from a plain program's by a relative error of at most 0.0008.
Values may be sent and summed in bfloat16 or wider, within the bound.
A program may use at most 128 MiB of HBM per device.

v0:
```python
import jax
import jax.numpy as jnp
from jax import lax
from jax.sharding import PartitionSpec as P


def dot_nt(a, b):
    return lax.dot_general(a, b, (((1,), (1,)), ((), ())), preferred_element_type=jnp.float32)


def dot_tn(a, b):
    return lax.dot_general(a, b, (((0,), (0,)), ((), ())), preferred_element_type=jnp.float32)


def weights(queries, qtangent, tail_rows, entities, etangent, ent_ids):
    score = dot_nt(queries, entities)
    dscore = dot_nt(qtangent, entities) + dot_nt(queries, etangent)
    prob = jax.nn.sigmoid(score)
    label = jnp.zeros(score.shape, jnp.float32)
    for k in range(tail_rows.shape[1]):
        label = jnp.maximum(
            label, (tail_rows[:, k : k + 1] == ent_ids[None, :]).astype(jnp.float32)
        )
    ugrad = (prob - label).astype(jnp.bfloat16)
    uhess = (prob * (1.0 - prob) * dscore).astype(jnp.bfloat16)
    return (uhess, ugrad)


def per_device(ent_emb, ent_tan, qry_emb, qry_tan, tails):
    ent_rows = ent_emb.shape[0]
    width = ent_emb.shape[1]
    panel_q, panel_dq = (
        lax.all_gather(qry_emb, "ent", axis=0, tiled=True),
        lax.all_gather(qry_tan, "ent", axis=0, tiled=True),
    )
    entities, etangent = (ent_emb, ent_tan)
    ent_ids = lax.axis_index("ent") * ent_rows + jnp.arange(ent_rows, dtype=jnp.int32)
    queries, qtangent, tail_rows = (panel_q, panel_dq, tails)
    uhess, ugrad = weights(queries, qtangent, tail_rows, entities, etangent, ent_ids)
    qrows = lax.psum_scatter(
        jnp.concatenate(
            [
                jnp.dot(uhess, entities, preferred_element_type=jnp.float32),
                jnp.dot(ugrad, entities, preferred_element_type=jnp.float32),
            ],
            axis=1,
        ),
        "ent",
        scatter_dimension=0,
        tiled=True,
    )
    erows = lax.psum_scatter(
        jnp.concatenate([dot_tn(uhess, queries), dot_tn(ugrad, queries)], axis=1),
        "qry",
        scatter_dimension=0,
        tiled=True,
    )
    return (erows[:, :width], erows[:, width:], qrows[:, :width], qrows[:, width:])


def solution(mesh):
    return jax.shard_map(
        per_device,
        mesh=mesh,
        in_specs=(
            P("ent", None),
            P("ent", None),
            P(("qry", "ent"), None),
            P(("qry", "ent"), None),
            P("qry", None),
        ),
        out_specs=(
            P(("ent", "qry"), None),
            P(("ent", "qry"), None),
            P(("qry", "ent"), None),
            P(("qry", "ent"), None),
        ),
        check_vma=False,
    )
```

profile of v0, /device:TPU:1, one launch (start us, length us, event | category | flops | bytes accessed | tf_op | source)
XLA Modules:
  0.0 606.4 jit_solution(13524694855700156160)
XLA Ops:
  7.2 0.0 copy-start
  7.2 0.0 all-gather.5.cloned.1.call-start
  7.2 0.7 all-gather.5.cloned.1.call-update
  7.9 0.0 all-gather.3.cloned.1.call-start
  8.0 0.7 all-gather.3.cloned.1.call-update
  8.7 0.0 reduce-scatter.7.cloned.1.call-start
  8.7 0.9 fusion.4
  9.6 132.4 %all-gather.5.cloned.1.call-done = bf16[1024,512]{1,0:T(8,128)(2,1)} async-done(((bf16[32,512]{1,0:T(8,128)(2,1)}), bf16[1024,512]{1,0:T(8,128)(2,1)}) %all-gather.5.cloned.1.call-update) | async-done | bytes 1048592 | tf_op jit(solution)/shard_map/all_gather | solution.py:34
  142.0 0.0 copy-done
  142.0 6.8 %fusion.5 = f32[1024,2048]{1,0:T(8,128)} fusion(bf16[1024,512]{1,0:T(8,128)(2,1)} %all-gather.5.cloned.1.call-done, bf16[2048,512]{1,0:T(8,128)(2,1)S(1)} %copy-done), kind=kOutput, calls=%fused_computation.11 | convolution fusion | flops 2147483648 | bytes 11534336 | tf_op jit(solution)/shard_map/dot_general | solution.py:8
  148.8 145.9 %all-gather.3.cloned.1.call-done = bf16[1024,512]{1,0:T(8,128)(2,1)} async-done(((bf16[32,512]{1,0:T(8,128)(2,1)}), bf16[1024,512]{1,0:T(8,128)(2,1)}) %all-gather.3.cloned.1.call-update) | async-done | bytes 1048592 | tf_op jit(solution)/shard_map/all_gather | solution.py:33
  294.7 8.4 %subtract_convert_fusion = (bf16[1024,2048]{1,0:T(8,128)(2,1)}, f32[1024,2048]{1,0:T(8,128)S(1)}) fusion(s32[2048]{0:T(1024)S(1)} %iota_add_fusion, s32[1024]{0:T(1024)S(1)} %bitcast.21, s32[1024]{0:T(1024)S(1)} %bitcast.22, s32[1024]{0:T(1024)S(1)} %bitcast.20, s32[1024]{0:T(1024)S(1)} %bitcast.19, bf16[1024,512]{1,0:T(8,128)(2,1)} %all-gather.3.cloned.1.call-done, ...), kind=kOutput, calls=%fused_computation.4 | convolution fusion | flops 2183135232 | bytes 15753216 | tf_op jit(solution)/shard_map/dot_general | solution.py:8
  303.1 6.5 %fusion.1 = bf16[1024,2048]{1,0:T(8,128)(2,1)} fusion(f32[1024,2048]{1,0:T(8,128)S(1)} %get-tuple-element.21, f32[1024,2048]{1,0:T(8,128)S(1)} %copy-done.2, bf16[1024,512]{1,0:T(8,128)(2,1)} %all-gather.3.cloned.1.call-done, bf16[2048,512]{1,0:T(8,128)(2,1)} %param.6), kind=kOutput, calls=%fused_computation.2 | convolution fusion | flops 2157969408 | bytes 24117248 | tf_op jit(solution)/shard_map/dot_general | solution.py:8
  309.7 4.7 fusion.8
  314.4 0.0 copy-done.4
  314.4 2.4 fusion.9
  316.8 2.5 pad_maximum_fusion.1
  319.3 5.4 copy.17
  324.7 0.0 reduce-scatter.7.cloned.1.call-update
  324.7 0.2 reduce-scatter.5.cloned.1.call-start
  324.9 1.0 copy-done.3
  325.9 4.7 fusion.6
  330.6 0.0 copy-done.5
  330.6 2.5 fusion.7
  333.1 3.8 pad_maximum_fusion
  336.9 0.0 reduce-scatter.5.cloned.1.call-update
  337.0 155.2 %reduce-scatter.7.cloned.1.call-done = f32[32,1024]{1,0:T(8,128)} async-done(((f32[1024,1024]{1,0:T(8,128)}), f32[32,1024]{1,0:T(8,128)}) %reduce-scatter.7.cloned.1.call-update) | async-done | bytes 131088
  492.2 1.7 fusion.3
  493.9 99.5 %reduce-scatter.5.cloned.1.call-done = f32[512,1024]{0,1:T(8,128)} async-done(((f32[2048,1024]{0,1:T(8,128)}), f32[512,1024]{0,1:T(8,128)}) %reduce-scatter.5.cloned.1.call-update) | async-done | bytes 2097168 | tf_op jit(solution)/shard_map/reduce_scatter | solution.py:52
  593.3 2.7 fusion.2
  596.0 2.5 copy.14
  598.5 1.3 copy.13
  (8 shorter events, 0.0 us)
Async XLA Ops:
  7.2 134.8 %copy-start = (bf16[2048,512]{1,0:T(8,128)(2,1)S(1)}, bf16[2048,512]{1,0:T(8,128)(2,1)}, u32[]{:S(2)}) copy-start(bf16[2048,512]{1,0:T(8,128)(2,1)} %param.5) | copy-start | bytes 6291460
  7.2 134.8 %all-gather.5.cloned.1.call-start = ((), (), s32[]{:S(2)}) async-start(), calls=%async_computation.3 | async-start | bytes 1081344 | tf_op jit(solution)/shard_map/all_gather | solution.py:34
  7.9 286.8 %all-gather.3.cloned.1.call-start = ((), (), s32[]{:S(2)}) async-start(), calls=%async_computation.2 | async-start | bytes 1081344 | tf_op jit(solution)/shard_map/all_gather | solution.py:33
  8.7 483.5 %reduce-scatter.7.cloned.1.call-start = ((), (), s32[]{:S(2)}) async-start(), calls=%async_computation.5 | async-start | bytes 4325376
  294.7 8.4 %copy-start.2 = (f32[1024,2048]{1,0:T(8,128)S(1)}, f32[1024,2048]{1,0:T(8,128)}, u32[]{:S(2)}) copy-start(f32[1024,2048]{1,0:T(8,128)} %fusion.5) | copy-start | bytes 25165828
  309.6 4.7 copy-start.4
  324.7 1.2 copy-start.3
  324.7 268.6 %reduce-scatter.5.cloned.1.call-start = ((), (), s32[]{:S(2)}) async-start(), calls=%async_computation.4 | async-start | bytes 10485760 | tf_op jit(solution)/shard_map/reduce_scatter | solution.py:52
  325.9 4.7 copy-start.5
  492.2 107.7 %copy-start.1 = (bf16[2048,512]{1,0:T(8,128)(2,1)S(1)}, bf16[2048,512]{1,0:T(8,128)(2,1)}, u32[]{:S(2)}) copy-start(bf16[2048,512]{1,0:T(8,128)(2,1)} %param.5) | copy-start | bytes 6291460
Sparse Core Ops, SparseCore 0:
  9.7 132.2 all-gather.4
  143.6 151.0 all-gather.2
  324.8 167.3 reduce-scatter.6
  494.7 98.5 reduce-scatter.4
where the time goes:
time: 607 us; the launch traced here: 606 us
  waiting for transfers between devices  534 us (88%)
  matrix products  36.1 us (6%)
  local copies, waits for them, and re-layouts  15.4 us (3%)
  between operations  13.8 us (2%)
  other arithmetic  6.33 us (1%)
    unnamed x5, waiting for transfers between devices  157 us
    all_gather x1, waiting for transfers between devices, per_device(): lax.all_gather(qry_emb, 'ent', axis=0, tiled=True)  146 us
    all_gather x1, waiting for transfers between devices, per_device(): lax.all_gather(qry_tan, 'ent', axis=0, tiled=True)  132 us
    reduce_scatter x1, waiting for transfers between devices, per_device(): lax.psum_scatter(jnp.concatenate([dot_tn(uhess, queries), dot_tn(ugrad, q...  99.5 us
    dot_general x3, matrix products, dot_nt(): lax.dot_general(a, b, (((1,), (1,)), ((), ())), preferred_element_type=jn...  21.7 us
  transfers between devices with their start and end apart: 4, of which 4 were waited for; matrix products, arithmetic and copies ran while one was open for 3% of the time, Pallas kernels for 0%

commit v1 on v0

--- a/solution.py
+++ b/solution.py
@@ -29,9 +29,16 @@
 def per_device(ent_emb, ent_tan, qry_emb, qry_tan, tails):
     ent_rows = ent_emb.shape[0]
     width = ent_emb.shape[1]
+
+    def produce_field_on_mesh(load, mesh_dim="ent"):
+        raw_out = jnp.stack(lax.axis_size(mesh_dim) * [load])
+        part_now = lax.all_to_all(raw_out, mesh_dim, 0, 0)
+        val2 = jnp.concatenate(part_now, axis=0)
+        return val2
+
     panel_q, panel_dq = (
         lax.all_gather(qry_emb, "ent", axis=0, tiled=True),
-        lax.all_gather(qry_tan, "ent", axis=0, tiled=True),
+        produce_field_on_mesh(qry_tan),
     )
     entities, etangent = (ent_emb, ent_tan)
     ent_ids = lax.axis_index("ent") * ent_rows + jnp.arange(ent_rows, dtype=jnp.int32)

time: 607 us -> 458 us (0.75)
  waiting for transfers between devices: 534 us -> 376 us
  starting transfers between devices: 0.34 us -> 10 us
    all_gather x1 -> x0, waiting for transfers between devices: 132 us -> none  [per_device(): lax.all_gather(qry_tan, 'ent', axis=0, tiled=True)]
    all_gather x1, waiting for transfers between devices: 146 us -> 106 us  [per_device(): lax.all_gather(qry_emb, 'ent', axis=0, tiled=True)]
    all_to_all x0 -> x1, waiting for transfers between devices: none -> 15.4 us  [produce_field_on_mesh(): part_now = lax.all_to_all(raw_out, mesh_dim, 0, 0)]
    all_to_all x0 -> x1, starting transfers between devices: none -> 9.73 us  [produce_field_on_mesh(): part_now = lax.all_to_all(raw_out, mesh_dim, 0, 0)]
    unnamed x5 -> x4, waiting for transfers between devices: 157 us -> 155 us
  transfers between devices with their start and end apart: 4 -> 4, of which waited for: 4 -> 4; matrix products, arithmetic and copies ran while one was open for 3% -> 5% of each run, Pallas kernels for 0% -> 0%
where the time goes in v1:
time: 458 us
  waiting for transfers between devices  376 us (82%)
  matrix products  34.8 us (8%)
  local copies, waits for them, and re-layouts  17.1 us (4%)
  between operations  13.8 us (3%)
  starting transfers between devices  10 us (2%)
  other arithmetic  6.31 us (1%)
    unnamed x4, waiting for transfers between devices  155 us
    all_gather x1, waiting for transfers between devices, per_device(): lax.all_gather(qry_emb, 'ent', axis=0, tiled=True)  106 us
    reduce_scatter x1, waiting for transfers between devices, per_device(): lax.psum_scatter(jnp.concatenate([dot_tn(uhess, queries), dot_tn(ugrad, q...  99.9 us
    dot_general x3, matrix products, dot_nt(): lax.dot_general(a, b, (((1,), (1,)), ((), ())), preferred_element_type=jn...  20.5 us
    all_to_all x1, waiting for transfers between devices, produce_field_on_mesh(): part_now = lax.all_to_all(raw_out, mesh_dim, 0, 0)  15.4 us
    unnamed x13, local copies, waits for them, and re-layouts  10.2 us
    all_to_all x1, starting transfers between devices, produce_field_on_mesh(): part_now = lax.all_to_all(raw_out, mesh_dim, 0, 0)  9.73 us
  transfers between devices with their start and end apart: 4, of which 4 were waited for; matrix products, arithmetic and copies ran while one was open for 5% of the time, Pallas kernels for 0%

profile of v1, /device:TPU:1, one launch (start us, length us, event | category | flops | bytes accessed | tf_op | source)
XLA Modules:
  0.0 457.7 jit_solution(6288747668821374540)
XLA Ops:
  7.2 0.0 copy-start
  7.2 0.0 all-gather.2.cloned.1.call-start
  7.2 0.7 all-gather.2.cloned.1.call-update
  7.9 1.8 stack.2
  9.8 9.7 %all-to-all-start = ((bf16[32,32,512]{2,1,0:T(8,128)(2,1)}), bf16[32,32,512]{2,1,0:T(8,128)(2,1)S(1)}, u32[]{:S(2)}, u32[]{:S(2)}) async-start(bf16[32,32,512]{2,1,0:T(8,128)(2,1)} %stack.2), calls=%async_computation | async-start | bytes 2097152 | tf_op jit(solution)/shard_map/all_to_all | solution.py:35
  19.5 0.0 reduce-scatter.7.cloned.1.call-start
  19.6 0.9 fusion.4
  20.5 15.4 %all-to-all-done = bf16[32,32,512]{2,1,0:T(8,128)(2,1)S(1)} async-done(((bf16[32,32,512]{2,1,0:T(8,128)(2,1)}), bf16[32,32,512]{2,1,0:T(8,128)(2,1)S(1)}, u32[]{:S(2)}, u32[]{:S(2)}) %all-to-all-start) | async-done | bytes 1048608 | tf_op jit(solution)/shard_map/all_to_all | solution.py:35
  35.8 0.0 copy-done
  35.8 5.6 %fusion.5 = f32[1024,2048]{1,0:T(8,128)} fusion(bf16[1024,512]{1,0:T(8,128)(2,1)S(1)} %bitcast.20, bf16[2048,512]{1,0:T(8,128)(2,1)S(1)} %copy-done), kind=kOutput, calls=%fused_computation.11 | convolution fusion | flops 2147483648 | bytes 11534336 | tf_op jit(solution)/shard_map/dot_general | solution.py:8
  41.4 105.5 %all-gather.2.cloned.1.call-done = bf16[1024,512]{1,0:T(8,128)(2,1)} async-done(((bf16[32,512]{1,0:T(8,128)(2,1)}), bf16[1024,512]{1,0:T(8,128)(2,1)}) %all-gather.2.cloned.1.call-update) | async-done | bytes 1048592 | tf_op jit(solution)/shard_map/all_gather | solution.py:40
  147.0 8.4 %subtract_convert_fusion = (bf16[1024,2048]{1,0:T(8,128)(2,1)}, f32[1024,2048]{1,0:T(8,128)S(1)}) fusion(s32[2048]{0:T(1024)S(1)} %iota_add_fusion, s32[1024]{0:T(1024)S(1)} %bitcast.23, s32[1024]{0:T(1024)S(1)} %bitcast.24, s32[1024]{0:T(1024)S(1)} %bitcast.22, s32[1024]{0:T(1024)S(1)} %bitcast.21, bf16[1024,512]{1,0:T(8,128)(2,1)} %all-gather.2.cloned.1.call-done, ...), kind=kOutput, calls=%fused_computation.4 | convolution fusion | flops 2183135232 | bytes 15753216 | tf_op jit(solution)/shard_map/dot_general | solution.py:8
  155.3 0.0 copy-done.1
  155.3 6.5 %fusion.1 = bf16[1024,2048]{1,0:T(8,128)(2,1)} fusion(f32[1024,2048]{1,0:T(8,128)S(1)} %get-tuple-element.21, f32[1024,2048]{1,0:T(8,128)S(1)} %copy-done.1, bf16[1024,512]{1,0:T(8,128)(2,1)} %all-gather.2.cloned.1.call-done, bf16[2048,512]{1,0:T(8,128)(2,1)} %param.6), kind=kOutput, calls=%fused_computation.2 | convolution fusion | flops 2157969408 | bytes 24117248 | tf_op jit(solution)/shard_map/dot_general | solution.py:8
  161.8 4.7 %fusion.8 = f32[1024,512]{0,1:T(8,128)S(1)} fusion(bf16[1024,2048]{1,0:T(8,128)(2,1)} %fusion.1, bf16[2048,512]{1,0:T(8,128)(2,1)S(1)} %copy-done), kind=kOutput, calls=%fused_computation.14 | convolution fusion | flops 2147483648 | bytes 8388608 | tf_op jit(solution)/shard_map/dot_general | solution.py:50
  166.5 0.0 copy-done.3
  166.6 2.4 fusion.9
  169.0 2.5 pad_maximum_fusion.1
  171.5 5.3 %copy.17 = f32[1024,1024]{1,0:T(8,128)} copy(f32[1024,1024]{0,1:T(8,128)} %pad_maximum_fusion.1) | data formatting | bytes 8388608
  176.8 0.0 reduce-scatter.7.cloned.1.call-update
  176.9 0.2 reduce-scatter.5.cloned.1.call-start
  177.1 1.0 copy-done.2
  178.1 4.7 %fusion.6 = f32[2048,512]{0,1:T(8,128)S(1)} fusion(bf16[1024,2048]{1,0:T(8,128)(2,1)} %fusion.1, bf16[1024,512]{1,0:T(8,128)(2,1)S(1)} %copy-done.2), kind=kOutput, calls=%fused_computation.12 | convolution fusion | flops 2147483648 | bytes 9437184 | tf_op jit(solution)/shard_map/dot_general | solution.py:12
  182.8 2.5 fusion.7
  185.3 3.8 pad_maximum_fusion
  189.1 0.0 reduce-scatter.5.cloned.1.call-update
  189.1 154.1 %reduce-scatter.7.cloned.1.call-done = f32[32,1024]{1,0:T(8,128)} async-done(((f32[1024,1024]{1,0:T(8,128)}), f32[32,1024]{1,0:T(8,128)}) %reduce-scatter.7.cloned.1.call-update) | async-done | bytes 131088
  343.2 1.5 fusion.3
  344.7 99.9 %reduce-scatter.5.cloned.1.call-done = f32[512,1024]{0,1:T(8,128)} async-done(((f32[2048,1024]{0,1:T(8,128)}), f32[512,1024]{0,1:T(8,128)}) %reduce-scatter.5.cloned.1.call-update) | async-done | bytes 2097168 | tf_op jit(solution)/shard_map/reduce_scatter | solution.py:59
  444.7 2.7 fusion.2
  447.3 2.5 copy.14
  449.9 1.3 copy.13
  (6 shorter events, 0.0 us)
Async XLA Ops:
  7.2 28.7 %copy-start = (bf16[2048,512]{1,0:T(8,128)(2,1)S(1)}, bf16[2048,512]{1,0:T(8,128)(2,1)}, u32[]{:S(2)}) copy-start(bf16[2048,512]{1,0:T(8,128)(2,1)} %param.5) | copy-start | bytes 6291460
  7.2 139.8 %all-gather.2.cloned.1.call-start = ((), (), s32[]{:S(2)}) async-start(), calls=%async_computation.3 | async-start | bytes 1081344 | tf_op jit(solution)/shard_map/all_gather | solution.py:40
  9.8 26.1 %all-to-all-start = ((bf16[32,32,512]{2,1,0:T(8,128)(2,1)}), bf16[32,32,512]{2,1,0:T(8,128)(2,1)S(1)}, u32[]{:S(2)}, u32[]{:S(2)}) async-start(bf16[32,32,512]{2,1,0:T(8,128)(2,1)} %stack.2), calls=%async_computation | async-start | bytes 2097152 | tf_op jit(solution)/shard_map/all_to_all | solution.py:35
  19.5 323.7 %reduce-scatter.7.cloned.1.call-start = ((), (), s32[]{:S(2)}) async-start(), calls=%async_computation.5 | async-start | bytes 4325376
  147.0 8.4 %copy-start.1 = (f32[1024,2048]{1,0:T(8,128)S(1)}, f32[1024,2048]{1,0:T(8,128)}, u32[]{:S(2)}) copy-start(f32[1024,2048]{1,0:T(8,128)} %fusion.5) | copy-start | bytes 25165828
  161.8 4.7 %copy-start.3 = (bf16[1024,2048]{1,0:T(8,128)(2,1)S(1)}, bf16[1024,2048]{1,0:T(8,128)(2,1)}, u32[]{:S(2)}) copy-start(bf16[1024,2048]{1,0:T(8,128)(2,1)} %get-tuple-element.20) | copy-start | bytes 12582916
  176.8 1.2 copy-start.2
  176.9 267.8 %reduce-scatter.5.cloned.1.call-start = ((), (), s32[]{:S(2)}) async-start(), calls=%async_computation.4 | async-start | bytes 10485760 | tf_op jit(solution)/shard_map/reduce_scatter | solution.py:59
  178.1 4.7 %copy-start.4 = (bf16[1024,2048]{1,0:T(8,128)(2,1)S(1)}, bf16[1024,2048]{1,0:T(8,128)(2,1)}, u32[]{:S(2)}) copy-start(bf16[1024,2048]{1,0:T(8,128)(2,1)} %get-tuple-element.20) | copy-start | bytes 12582916
Sparse Core Ops, SparseCore 0:
  9.7 137.2 all-gather.1
  177.0 166.1 reduce-scatter.6
  345.9 98.7 reduce-scatter.4
